TPU v7x, 256 devices: a whole 4x4x8 slice. The times are simulated.
256 devices in a mesh: section: 4 (over x), tp: 64 (over y, z, core).
Axes of the slice: x: 4, y: 4, z: 8, core: 2. Of those that a mesh axis runs over, the one named last changes fastest.
Arguments:
- tokens: bfloat16 [64, 8192], P(None, 'tp'), may hold values from -6 to 6
- norm_gain: float32 [4, 8192], P('section'), may hold values from 0.1 to 1.9
- gate_weight: bfloat16 [4, 8192, 16384], P('section', None, 'tp'), may hold values from -0.09375 to 0.09375
- up_weight: bfloat16 [4, 8192, 16384], P('section', None, 'tp'), may hold values from -0.09375 to 0.09375
- gate_mask: int32 [4, 128, 256], P('section', None, 'tp'), may hold values 0 or 1
- up_mask: int32 [4, 128, 256], P('section', None, 'tp'), may hold values 0 or 1
- down_weight: bfloat16 [4, 16384, 8192], P('section', 'tp'), may hold values from -0.125 to 0.125
- down_mask: int32 [4, 256, 128], P('section', 'tp'), may hold values 0 or 1
- slot_order: int32 [4, 256], P('section', 'tp'), may hold values from 0 to 255, as said below
Outputs:
- received: bfloat16 [4, 64, 8192], P('section', None, 'tp')
Inputs may be any that keep to these rules, and one draw needn't show every extreme that they name: `slot_order`: for each section a permutation of the 256 hidden blocks. Slot k lies on tp device k // 4; block b is computed on tp device b // 4. The slots of tp device t take exactly 1 block from each of the tp devices t, t + 1, ..., t + 4 - 1 (mod 64) and none from others. `gate_mask`: 1 keeps a block, 0 prunes it. `up_mask`: 1 keeps a block, 0 prunes it. `down_mask`: 1 keeps a block, 0 prunes it.
All inputs are finite; a program needn't handle non-finite values.
Results may differ from a plain program's by a relative error of at most 0.014.
Values may be sent and summed in bfloat16 or wider, within the bound.
A program may use at most 128 MiB of HBM per device.

v0:
```python
import jax
import jax.numpy as jnp
from jax import lax
from jax.sharding import PartitionSpec as P


def passed_along(block, axis, distance):
    devices = range(lax.axis_size(axis))
    route = [((i - distance) % len(devices), i) for i in devices]
    return lax.ppermute(block, axis, route)


def expand_mask(mask, width):
    return jnp.repeat(jnp.repeat(mask, width, axis=0), width, axis=1)


def masked(weight, mask, width):
    return weight * expand_mask(mask, width).astype(jnp.bfloat16)


def body(
    tokens,
    norm_gain,
    gate_weight,
    up_weight,
    gate_mask,
    up_mask,
    down_weight,
    down_mask,
    slot_order,
):
    sections = lax.axis_size("section")
    tp_count = lax.axis_size("tp")
    section_pos = lax.axis_index("section")
    tp_pos = lax.axis_index("tp")
    width = gate_weight.shape[1] // gate_mask.shape[1]
    w_gate = masked(gate_weight[0], gate_mask[0], width)
    w_up = masked(up_weight[0], up_mask[0], width)
    w_down = masked(down_weight[0], down_mask[0], width)
    gain = norm_gain[0]
    my_blocks = slot_order[0]
    per_device = my_blocks.shape[0]
    row_count, own_cols = tokens.shape
    window = min(tp_count, per_device)
    capacity = per_device // window
    slot_ids = jnp.arange(capacity, dtype=jnp.int32)
    my_source = my_blocks // per_device
    my_offset = (my_source - tp_pos) % tp_count
    lanes = jnp.arange(per_device, dtype=jnp.int32)
    earlier = (my_source[None, :] == my_source[:, None]) & (lanes[None, :] < lanes[:, None])
    my_rank = jnp.sum(earlier.astype(jnp.int32), axis=1)
    send_lists = []
    for offset in range(window):
        if offset == 0:
            table_row = my_blocks
        else:
            table_row = passed_along(my_blocks, "tp", offset)
        row_source = table_row // per_device
        row_block = table_row % per_device
        from_me = (row_source == tp_pos).astype(jnp.int32)
        order_rank = jnp.cumsum(from_me) - 1
        picks = (from_me[None, :] == 1) & (order_rank[None, :] == slot_ids[:, None])
        send_lists.append(jnp.sum(jnp.where(picks, row_block[None, :], 0), axis=1))
    x_full = lax.all_gather(tokens, "tp", axis=1, tiled=True)
    saved = jnp.zeros((row_count, own_cols), jnp.bfloat16)
    for round_pos in range(sections):
        x_own = lax.dynamic_slice_in_dim(x_full, tp_pos * own_cols, own_cols, 1)
        widened = x_full.astype(jnp.float32)
        scale = lax.rsqrt(jnp.mean(widened * widened, axis=-1, keepdims=True) + 1e-05)
        normed = (widened * scale * gain).astype(jnp.bfloat16)
        gate = jnp.dot(normed, w_gate, preferred_element_type=jnp.float32)
        upper = jnp.dot(normed, w_up, preferred_element_type=jnp.float32)
        hidden = (jax.nn.silu(gate) * upper).astype(jnp.bfloat16)
        flat = (
            hidden.reshape(row_count, per_device, width)
            .transpose(1, 0, 2)
            .reshape(per_device, row_count * width)
        )
        arrivals = []
        for gather_offset in range(window):
            outgoing = flat[send_lists[gather_offset]]
            if gather_offset == 0:
                arrivals.append(outgoing)
            else:
                arrivals.append(passed_along(outgoing, "tp", tp_count - gather_offset))
        stacked = jnp.stack(arrivals)
        chosen = stacked[my_offset, my_rank]
        mine = (
            chosen.reshape(per_device, row_count, width)
            .transpose(1, 0, 2)
            .reshape(row_count, per_device * width)
        )
        partial_sum = jnp.dot(mine, w_down, preferred_element_type=jnp.float32)
        summed = lax.psum_scatter(partial_sum, "tp", scatter_dimension=1, tiled=True)
        y_own = (x_own.astype(jnp.float32) + summed).astype(jnp.bfloat16)
        section_full = lax.all_gather(y_own, "tp", axis=1, tiled=True)
        x_full = passed_along(section_full, "section", 1)
        got_own = lax.dynamic_slice_in_dim(x_full, tp_pos * own_cols, own_cols, 1)
        saved = jnp.where(section_pos == (round_pos + 1) % sections, got_own, saved)
    return saved[None]


def solution(mesh):
    return jax.shard_map(
        body,
        mesh=mesh,
        in_specs=(
            P(None, "tp"),
            P("section", None),
            P("section", None, "tp"),
            P("section", None, "tp"),
            P("section", None, "tp"),
            P("section", None, "tp"),
            P("section", "tp", None),
            P("section", "tp", None),
            P("section", "tp"),
        ),
        out_specs=P("section", None, "tp"),
        check_vma=False,
    )
```

profile of v0, /device:TPU:1, one launch (start us, length us, event | category | flops | bytes accessed | tf_op | source)
XLA Modules:
  0.0 1125.9 jit_solution(15061843299415078217)
XLA Ops:
  6.5 3.0 collective-permute-start
  9.6 1.6 collective-permute-start.2
  11.2 1.7 collective-permute-start.4
  16.4 6.4 copy.36
  23.1 6.4 copy.37
  30.5 4.6 bitcast_multiply_fusion.2
  35.1 2.3 bitcast_multiply_fusion.1
  46.1 38.5 %all-gather.6.cloned.1.call-done = bf16[64,8192]{1,0:T(8,128)(2,1)} async-done(((bf16[64,128]{1,0:T(8,128)(2,1)}), bf16[64,8192]{1,0:T(8,128)(2,1)}) %all-gather.6.cloned.1.call-update) | async-done | bytes 1048592 | tf_op jit(solution)/shard_map/all_gather | solution.py:64
  84.6 1.5 fusion.8
  86.2 4.1 fusion.34
  90.2 1.4 fusion.20
  92.3 4.3 collective-permute-start.3
  96.6 1.9 collective-permute-start.5
  98.5 6.4 copy.41
  105.0 4.4 bitcast_multiply_fusion
  110.6 4.9 fusion.6
  115.6 130.5 %reduce-scatter.5.cloned.1.call-done = f32[64,128]{1,0:T(8,128)} async-done(((f32[64,8192]{1,0:T(8,128)}), f32[64,128]{1,0:T(8,128)}) %reduce-scatter.5.cloned.1.call-update) | async-done | bytes 32784 | tf_op jit(solution)/shard_map/reduce_scatter | solution.py:94
  246.0 1.4 add_convert_fusion.3
  247.5 76.0 %all-gather.8.cloned.1.call-done = bf16[64,8192]{1,0:T(8,128)(2,1)} async-done(((bf16[64,128]{1,0:T(8,128)(2,1)}), bf16[64,8192]{1,0:T(8,128)(2,1)}) %all-gather.8.cloned.1.call-update) | async-done | bytes 1048592 | tf_op jit(solution)/shard_map/all_gather | solution.py:96
  324.5 24.8 %collective-permute-done.6 = bf16[64,8192]{1,0:T(8,128)(2,1)S(1)} collective-permute-done((bf16[64,8192]{1,0:T(8,128)(2,1)}, bf16[64,8192]{1,0:T(8,128)(2,1)S(1)}, u32[]{:S(2)}, u32[]{:S(2)}) %collective-permute-start.6) | collective-permute-done | bytes 1048608 | tf_op jit(solution)/shard_map/ppermute | solution.py:10
  349.7 3.7 fusion.31
  353.5 1.4 multiply_convert_fusion.2
  356.4 4.3 collective-permute-start.8
  361.7 3.0 collective-permute-done.9
  365.8 4.9 fusion.4
  370.8 132.0 %reduce-scatter.7.cloned.1.call-done = f32[64,128]{1,0:T(8,128)} async-done(((f32[64,8192]{1,0:T(8,128)}), f32[64,128]{1,0:T(8,128)}) %reduce-scatter.7.cloned.1.call-update) | async-done | bytes 32784 | tf_op jit(solution)/shard_map/reduce_scatter | solution.py:94
  502.8 1.4 add_convert_fusion.2
  504.2 75.2 %all-gather.10.cloned.1.call-done = bf16[64,8192]{1,0:T(8,128)(2,1)} async-done(((bf16[64,128]{1,0:T(8,128)(2,1)}), bf16[64,8192]{1,0:T(8,128)(2,1)}) %all-gather.10.cloned.1.call-update) | async-done | bytes 1048592 | tf_op jit(solution)/shard_map/all_gather | solution.py:96
  580.5 24.8 %collective-permute-done.10 = bf16[64,8192]{1,0:T(8,128)(2,1)S(1)} collective-permute-done((bf16[64,8192]{1,0:T(8,128)(2,1)}, bf16[64,8192]{1,0:T(8,128)(2,1)S(1)}, u32[]{:S(2)}, u32[]{:S(2)}) %collective-permute-start.10) | collective-permute-done | bytes 1048608 | tf_op jit(solution)/shard_map/ppermute | solution.py:10
  605.7 3.7 fusion.27
  609.4 1.4 multiply_convert_fusion.1
  612.3 4.3 collective-permute-start.12
  617.7 3.0 collective-permute-done.13
  621.8 4.9 fusion.2
  626.8 132.0 %reduce-scatter.9.cloned.1.call-done = f32[64,128]{1,0:T(8,128)} async-done(((f32[64,8192]{1,0:T(8,128)}), f32[64,128]{1,0:T(8,128)}) %reduce-scatter.9.cloned.1.call-update) | async-done | bytes 32784 | tf_op jit(solution)/shard_map/reduce_scatter | solution.py:94
  758.8 1.4 add_convert_fusion.1
  760.2 75.6 %all-gather.12.cloned.1.call-done = bf16[64,8192]{1,0:T(8,128)(2,1)} async-done(((bf16[64,128]{1,0:T(8,128)(2,1)}), bf16[64,8192]{1,0:T(8,128)(2,1)}) %all-gather.12.cloned.1.call-update) | async-done | bytes 1048592 | tf_op jit(solution)/shard_map/all_gather | solution.py:96
  837.0 24.8 %collective-permute-done.14 = bf16[64,8192]{1,0:T(8,128)(2,1)S(1)} collective-permute-done((bf16[64,8192]{1,0:T(8,128)(2,1)}, bf16[64,8192]{1,0:T(8,128)(2,1)S(1)}, u32[]{:S(2)}, u32[]{:S(2)}) %collective-permute-start.14) | collective-permute-done | bytes 1048608 | tf_op jit(solution)/shard_map/ppermute | solution.py:10
  862.1 3.7 fusion.23
  865.9 1.4 multiply_convert_fusion
  868.8 4.3 collective-permute-start.16
  874.2 3.0 collective-permute-done.17
  878.2 4.9 fusion
  883.2 132.0 %reduce-scatter.11.cloned.1.call-done = f32[64,128]{1,0:T(8,128)} async-done(((f32[64,8192]{1,0:T(8,128)}), f32[64,128]{1,0:T(8,128)}) %reduce-scatter.11.cloned.1.call-update) | async-done | bytes 32784 | tf_op jit(solution)/shard_map/reduce_scatter | solution.py:94
  1015.2 1.4 add_convert_fusion
  1016.6 75.4 %all-gather.14.cloned.1.call-done = bf16[64,8192]{1,0:T(8,128)(2,1)} async-done(((bf16[64,128]{1,0:T(8,128)(2,1)}), bf16[64,8192]{1,0:T(8,128)(2,1)}) %all-gather.14.cloned.1.call-update) | async-done | bytes 1048592 | tf_op jit(solution)/shard_map/all_gather | solution.py:96
  1093.1 24.9 %collective-permute-done.18 = bf16[64,8192]{1,0:T(8,128)(2,1)} collective-permute-done((bf16[64,8192]{1,0:T(8,128)(2,1)}, bf16[64,8192]{1,0:T(8,128)(2,1)}, u32[]{:S(2)}, u32[]{:S(2)}) %collective-permute-start.18) | collective-permute-done | bytes 1048608 | tf_op jit(solution)/shard_map/ppermute | solution.py:10
  1118.0 1.3 select_bitcast_fusion
  (130 shorter events, 24.0 us)
Async XLA Ops:
  6.5 78.0 %all-gather.6.cloned.1.call-start = ((), (), s32[]{:S(2)}) async-start(), calls=%async_computation.4 | async-start | bytes 1064960 | tf_op jit(solution)/shard_map/all_gather | solution.py:64
  6.5 31.1 %collective-permute-start = (s32[4]{0:T(128)}, s32[4]{0:T(128)S(1)}, u32[]{:S(2)}, u32[]{:S(2)}) collective-permute-start(s32[4]{0:T(128)} %bitcast.171), channel_id=1, source_target_pairs={{63,0},{0,1},{1,2},{2,3},{3,4},{4,5},{5,6},{6,7},{7,8},{8,9},{9,10... | collective-permute-start | bytes 56 | tf_op jit(solution)/shard_map/ppermute | solution.py:10
  9.6 30.2 %collective-permute-start.2 = (s32[4]{0:T(128)}, s32[4]{0:T(128)S(1)}, u32[]{:S(2)}, u32[]{:S(2)}) collective-permute-start(s32[4]{0:T(128)} %bitcast.172), channel_id=1, source_target_pairs={{62,0},{63,1},{0,2},{1,3},{2,4},{3,5},{4,6},{5,7},{6,8},{7,9},{8,1... | collective-permute-start | bytes 56 | tf_op jit(solution)/shard_map/ppermute | solution.py:10
  11.2 30.8 %collective-permute-start.4 = (s32[4]{0:T(128)}, s32[4]{0:T(128)S(1)}, u32[]{:S(2)}, u32[]{:S(2)}) collective-permute-start(s32[4]{0:T(128)} %bitcast.173), channel_id=1, source_target_pairs={{61,0},{62,1},{63,2},{0,3},{1,4},{2,5},{3,6},{4,7},{5,8},{6,9},{7,... | collective-permute-start | bytes 56 | tf_op jit(solution)/shard_map/ppermute | solution.py:10
  12.9 233.1 %reduce-scatter.5.cloned.1.call-start = ((), (), s32[]{:S(2)}) async-start(), calls=%async_computation.5 | async-start | bytes 2129920 | tf_op jit(solution)/shard_map/reduce_scatter | solution.py:94
  16.4 6.4 copy-start.8
  23.1 6.4 copy-start.9
  30.5 4.6 copy-start.4
  35.1 2.3 copy-start.7
  35.1 2.5 copy-start.10
  35.1 51.0 %copy-start.6 = (f32[1,8192]{1,0:T(1,128)S(1)}, f32[1,8192]{1,0:T(1,128)}, u32[]{:S(2)}) copy-start(f32[1,8192]{1,0:T(1,128)} %param.10) | copy-start | bytes 98308
  86.1 4.1 copy-start
  86.1 4.1 copy-start.5
  92.0 17.5 %collective-permute-start.1 = (bf16[1,4096]{1,0:T(2,128)(2,1)S(1)}, bf16[1,4096]{1,0:T(2,128)(2,1)S(1)}, u32[]{:S(2)}, u32[]{:S(2)}) collective-permute-start(bf16[1,4096]{1,0:T(2,128)(2,1)S(1)} %get-tuple-element.198), channel_id=1, source_target_pairs={{1,0},{2,1},{3,2},{4,3},{5,4},{6,5},{7,6},{8,7},{9,8},{10,9},{11,1... | collective-permute-start | bytes 24584 | tf_op jit(solution)/shard_map/ppermute | solution.py:10
  92.3 17.2 %collective-permute-start.3 = (bf16[1,4096]{1,0:T(2,128)(2,1)S(1)}, bf16[1,4096]{1,0:T(2,128)(2,1)S(1)}, u32[]{:S(2)}, u32[]{:S(2)}) collective-permute-start(bf16[1,4096]{1,0:T(2,128)(2,1)S(1)} %get-tuple-element.197), channel_id=1, source_target_pairs={{2,0},{3,1},{4,2},{5,3},{6,4},{7,5},{8,6},{9,7},{10,8},{11,9},{12,... | collective-permute-start | bytes 24584 | tf_op jit(solution)/shard_map/ppermute | solution.py:10
  96.6 12.9 %collective-permute-start.5 = (bf16[1,4096]{1,0:T(2,128)(2,1)S(1)}, bf16[1,4096]{1,0:T(2,128)(2,1)S(1)}, u32[]{:S(2)}, u32[]{:S(2)}) collective-permute-start(bf16[1,4096]{1,0:T(2,128)(2,1)S(1)} %get-tuple-element.196), channel_id=1, source_target_pairs={{3,0},{4,1},{5,2},{6,3},{7,4},{8,5},{9,6},{10,7},{11,8},{12,9},{13... | collective-permute-start | bytes 24584 | tf_op jit(solution)/shard_map/ppermute | solution.py:10
  115.5 207.9 %all-gather.8.cloned.1.call-start = ((), (), s32[]{:S(2)}) async-start(), calls=%async_computation.6 | async-start | bytes 1064960 | tf_op jit(solution)/shard_map/all_gather | solution.py:96
  247.4 255.4 %reduce-scatter.7.cloned.1.call-start = ((), (), s32[]{:S(2)}) async-start(), calls=%async_computation.7 | async-start | bytes 2129920 | tf_op jit(solution)/shard_map/reduce_scatter | solution.py:94
  323.4 25.9 %collective-permute-start.6 = (bf16[64,8192]{1,0:T(8,128)(2,1)}, bf16[64,8192]{1,0:T(8,128)(2,1)S(1)}, u32[]{:S(2)}, u32[]{:S(2)}) collective-permute-start(bf16[64,8192]{1,0:T(8,128)(2,1)} %all-gather.8.cloned.1.call-done), channel_id=1, source_target_pairs={{192,0},{0,64},{64,128},{128,192},{193,1},{1,65},{65,129},{129,193... | collective-permute-start | bytes 3145736 | tf_op jit(solution)/shard_map/ppermute | solution.py:10
  349.7 3.8 copy-start.1
  355.2 6.5 collective-permute-start.7
  356.4 5.4 collective-permute-start.8
  360.7 4.1 collective-permute-start.9
  370.7 208.7 %all-gather.10.cloned.1.call-start = ((), (), s32[]{:S(2)}) async-start(), calls=%async_computation.8 | async-start | bytes 1064960 | tf_op jit(solution)/shard_map/all_gather | solution.py:96
  504.2 254.6 %reduce-scatter.9.cloned.1.call-start = ((), (), s32[]{:S(2)}) async-start(), calls=%async_computation.9 | async-start | bytes 2129920 | tf_op jit(solution)/shard_map/reduce_scatter | solution.py:94
  579.4 25.9 %collective-permute-start.10 = (bf16[64,8192]{1,0:T(8,128)(2,1)}, bf16[64,8192]{1,0:T(8,128)(2,1)S(1)}, u32[]{:S(2)}, u32[]{:S(2)}) collective-permute-start(bf16[64,8192]{1,0:T(8,128)(2,1)} %all-gather.10.cloned.1.call-done), channel_id=1, source_target_pairs={{192,0},{0,64},{64,128},{128,192},{193,1},{1,65},{65,129},{129,193... | collective-permute-start | bytes 3145736 | tf_op jit(solution)/shard_map/ppermute | solution.py:10
  605.7 3.8 copy-start.2
  611.2 6.5 collective-permute-start.11
  612.3 5.4 collective-permute-start.12
  616.6 4.1 collective-permute-start.13
  626.7 209.2 %all-gather.12.cloned.1.call-start = ((), (), s32[]{:S(2)}) async-start(), calls=%async_computation.10 | async-start | bytes 1064960 | tf_op jit(solution)/shard_map/all_gather | solution.py:96
  760.2 255.0 %reduce-scatter.11.cloned.1.call-start = ((), (), s32[]{:S(2)}) async-start(), calls=%async_computation.11 | async-start | bytes 2129920 | tf_op jit(solution)/shard_map/reduce_scatter | solution.py:94
  835.9 25.9 %collective-permute-start.14 = (bf16[64,8192]{1,0:T(8,128)(2,1)}, bf16[64,8192]{1,0:T(8,128)(2,1)S(1)}, u32[]{:S(2)}, u32[]{:S(2)}) collective-permute-start(bf16[64,8192]{1,0:T(8,128)(2,1)} %all-gather.12.cloned.1.call-done), channel_id=1, source_target_pairs={{192,0},{0,64},{64,128},{128,192},{193,1},{1,65},{65,129},{129,193... | collective-permute-start | bytes 3145736 | tf_op jit(solution)/shard_map/ppermute | solution.py:10
  862.1 3.8 copy-start.3
  867.6 6.5 collective-permute-start.15
  868.8 5.4 collective-permute-start.16
  873.1 4.1 collective-permute-start.17
  883.2 208.8 %all-gather.14.cloned.1.call-start = ((), (), s32[]{:S(2)}) async-start(), calls=%async_computation.12 | async-start | bytes 1064960 | tf_op jit(solution)/shard_map/all_gather | solution.py:96
  1092.0 26.0 %collective-permute-start.18 = (bf16[64,8192]{1,0:T(8,128)(2,1)}, bf16[64,8192]{1,0:T(8,128)(2,1)}, u32[]{:S(2)}, u32[]{:S(2)}) collective-permute-start(bf16[64,8192]{1,0:T(8,128)(2,1)} %all-gather.14.cloned.1.call-done), channel_id=1, source_target_pairs={{192,0},{0,64},{64,128},{128,192},{193,1},{1,65},{65,129},{129,193... | collective-permute-start | bytes 3145736 | tf_op jit(solution)/shard_map/ppermute | solution.py:10
Sparse Core Ops, SparseCore 0:
  13.0 71.5 all-gather.5
  115.6 130.3 reduce-scatter.4
  248.9 74.4 all-gather.7
  370.9 131.9 reduce-scatter.6
  505.2 74.1 all-gather.9
  626.8 131.9 reduce-scatter.8
  761.7 74.1 all-gather.11
  883.3 131.9 reduce-scatter.10
  1017.8 74.1 all-gather.13
where the time goes:
time: 1130 us
  waiting for transfers between devices  976 us (86%)
  matrix products  40.5 us (4%)
  starting transfers between devices  37.1 us (3%)
  other arithmetic  25.9 us (2%)
  local copies, waits for them, and re-layouts  25.1 us (2%)
  between operations  21.4 us (2%)
    reduce_scatter x4, waiting for transfers between devices, body(): lax.psum_scatter(partial_sum, 'tp', scatter_dimension=1, tiled=True)  527 us
    all_gather x4, waiting for transfers between devices, body(): section_full = lax.all_gather(y_own, 'tp', axis=1, tiled=True)  302 us
    ppermute x19, waiting for transfers between devices, passed_along(): return lax.ppermute(block, axis, route)  108 us
    all_gather x1, waiting for transfers between devices, body(): x_full = lax.all_gather(tokens, 'tp', axis=1, tiled=True)  38.5 us
    ppermute x19, starting transfers between devices, passed_along(): return lax.ppermute(block, axis, route)  36.8 us
  transfers between devices with their start and end apart: 28, of which 16 were waited for; matrix products, arithmetic and copies ran while one was open for 3% of the time, Pallas kernels for 0%

commit v1 on v0

--- a/solution.py
+++ b/solution.py
@@ -93,7 +93,9 @@
         partial_sum = jnp.dot(mine, w_down, preferred_element_type=jnp.float32)
         summed = lax.psum_scatter(partial_sum, "tp", scatter_dimension=1, tiled=True)
         y_own = (x_own.astype(jnp.float32) + summed).astype(jnp.bfloat16)
-        section_full = lax.all_gather(y_own, "tp", axis=1, tiled=True)
+        section_full = jnp.concatenate(
+            lax.all_to_all(jnp.stack([y_own] * lax.axis_size("tp")), "tp", 0, 0), axis=1
+        )
         x_full = passed_along(section_full, "section", 1)
         got_own = lax.dynamic_slice_in_dim(x_full, tp_pos * own_cols, own_cols, 1)
         saved = jnp.where(section_pos == (round_pos + 1) % sections, got_own, saved)

time: 1130 us -> 986 us (0.87)
  waiting for transfers between devices: 976 us -> 672 us
  blocking collectives: 0 us -> 166 us
    all_gather x4 -> x0, waiting for transfers between devices: 302 us -> none  [body(): section_full = lax.all_gather(y_own, 'tp', axis=1, tiled=True)]
    all_to_all x0 -> x4, blocking collectives: none -> 166 us  [body(): lax.all_to_all(jnp.stack([y_own] * lax.axis_size('tp')), 'tp', 0, 0)]
  transfers between devices with their start and end apart: 28 -> 24, of which waited for: 16 -> 12; matrix products, arithmetic and copies ran while one was open for 3% -> 4% of each run, Pallas kernels for 0% -> 0%
where the time goes in v1:
time: 986 us; the launch traced here: 977 us
  waiting for transfers between devices  672 us (68%)
  blocking collectives  166 us (17%)
  matrix products  33.6 us (3%)
  local copies, waits for them, and re-layouts  29.9 us (3%)
  starting transfers between devices  29.2 us (3%)
  other arithmetic  23.5 us (2%)
  between operations  21.8 us (2%)
    reduce_scatter x4, waiting for transfers between devices, body(): lax.psum_scatter(partial_sum, 'tp', scatter_dimension=1, tiled=True)  525 us
    all_to_all x4, blocking collectives, body(): lax.all_to_all(jnp.stack([y_own] * lax.axis_size('tp')), 'tp', 0, 0)  166 us
    ppermute x19, waiting for transfers between devices, passed_along(): return lax.ppermute(block, axis, route)  108 us
    all_gather x1, waiting for transfers between devices, body(): x_full = lax.all_gather(tokens, 'tp', axis=1, tiled=True)  38.5 us
    ppermute x19, starting transfers between devices, passed_along(): return lax.ppermute(block, axis, route)  29.1 us
    unnamed x31, local copies, waits for them, and re-layouts  21.5 us
  transfers between devices with their start and end apart: 24, of which 12 were waited for; matrix products, arithmetic and copies ran while one was open for 4% of the time, Pallas kernels for 0%

profile of v1, /device:TPU:1, one launch (start us, length us, event | category | flops | bytes accessed | tf_op | source)
XLA Modules:
  0.0 976.5 jit_solution(18155442855897687632)
XLA Ops:
  6.5 3.0 collective-permute-start
  9.6 1.6 collective-permute-start.2
  11.2 1.7 collective-permute-start.4
  13.8 1.3 fusion.47
  16.4 6.4 copy.52
  23.1 6.5 copy.53
  30.5 4.6 bitcast_multiply_fusion.2
  35.1 2.3 bitcast_multiply_fusion.1
  46.1 38.5 %all-gather.2.cloned.1.call-done = bf16[64,8192]{1,0:T(8,128)(2,1)} async-done(((bf16[64,128]{1,0:T(8,128)(2,1)}), bf16[64,8192]{1,0:T(8,128)(2,1)}) %all-gather.2.cloned.1.call-update) | async-done | bytes 1048592 | tf_op jit(solution)/shard_map/all_gather | solution.py:64
  84.6 1.5 fusion.8
  86.2 4.1 fusion.34
  90.2 1.4 fusion.20
  92.3 4.3 collective-permute-start.3
  96.6 1.9 collective-permute-start.5
  98.5 6.4 copy.57
  105.0 4.4 bitcast_multiply_fusion
  110.6 4.9 fusion.6
  115.6 130.8 %reduce-scatter.5.cloned.1.call-done = f32[64,128]{1,0:T(8,128)} async-done(((f32[64,8192]{1,0:T(8,128)}), f32[64,128]{1,0:T(8,128)}) %reduce-scatter.5.cloned.1.call-update) | async-done | bytes 32784 | tf_op jit(solution)/shard_map/reduce_scatter | solution.py:94
  247.4 41.4 %all_to_all.20 = bf16[64,64,128]{2,1,0:T(8,128)(2,1)S(1)} all-to-all(bf16[64,64,128]{2,1,0:T(8,128)(2,1)S(1)} %stack.53), channel_id=1, replica_groups=mesh['section'=4,'tp'=64] {'tp'}, dimensions={0} | all-to-all | bytes 2097152 | tf_op jit(solution)/shard_map/all_to_all | solution.py:97
  288.9 1.3 collective-permute-start.6
  290.2 24.7 %collective-permute-done.6 = bf16[64,8192]{1,0:T(8,128)(2,1)S(1)} collective-permute-done((bf16[64,8192]{1,0:T(8,128)(2,1)S(1)}, bf16[64,8192]{1,0:T(8,128)(2,1)S(1)}, u32[]{:S(2)}, u32[]{:S(2)}) %collective-permute-start.6) | collective-permute-done | bytes 1048608 | tf_op jit(solution)/shard_map/ppermute | solution.py:10
  315.3 1.4 fusion.31
  317.5 1.4 multiply_convert_fusion.2
  320.1 1.6 collective-permute-start.8
  322.9 3.0 collective-permute-done.9
  326.9 4.9 fusion.4
  331.9 131.5 %reduce-scatter.7.cloned.1.call-done = f32[64,128]{1,0:T(8,128)} async-done(((f32[64,8192]{1,0:T(8,128)}), f32[64,128]{1,0:T(8,128)}) %reduce-scatter.7.cloned.1.call-update) | async-done | bytes 32784 | tf_op jit(solution)/shard_map/reduce_scatter | solution.py:94
  464.5 41.7 %all_to_all.21 = bf16[64,64,128]{2,1,0:T(8,128)(2,1)S(1)} all-to-all(bf16[64,64,128]{2,1,0:T(8,128)(2,1)S(1)} %stack.59), channel_id=1, replica_groups=mesh['section'=4,'tp'=64] {'tp'}, dimensions={0} | all-to-all | bytes 2097152 | tf_op jit(solution)/shard_map/all_to_all | solution.py:97
  506.3 1.3 collective-permute-start.10
  507.6 24.7 %collective-permute-done.10 = bf16[64,8192]{1,0:T(8,128)(2,1)S(1)} collective-permute-done((bf16[64,8192]{1,0:T(8,128)(2,1)S(1)}, bf16[64,8192]{1,0:T(8,128)(2,1)S(1)}, u32[]{:S(2)}, u32[]{:S(2)}) %collective-permute-start.10) | collective-permute-done | bytes 1048608 | tf_op jit(solution)/shard_map/ppermute | solution.py:10
  532.6 1.4 fusion.27
  534.8 1.4 multiply_convert_fusion.1
  537.7 1.6 collective-permute-start.12
  540.5 3.0 collective-permute-done.13
  544.5 4.9 fusion.2
  549.5 131.5 %reduce-scatter.9.cloned.1.call-done = f32[64,128]{1,0:T(8,128)} async-done(((f32[64,8192]{1,0:T(8,128)}), f32[64,128]{1,0:T(8,128)}) %reduce-scatter.9.cloned.1.call-update) | async-done | bytes 32784 | tf_op jit(solution)/shard_map/reduce_scatter | solution.py:94
  682.0 41.7 %all_to_all.22 = bf16[64,64,128]{2,1,0:T(8,128)(2,1)S(1)} all-to-all(bf16[64,64,128]{2,1,0:T(8,128)(2,1)S(1)} %stack.65), channel_id=1, replica_groups=mesh['section'=4,'tp'=64] {'tp'}, dimensions={0} | all-to-all | bytes 2097152 | tf_op jit(solution)/shard_map/all_to_all | solution.py:97
  723.8 1.3 collective-permute-start.14
  725.1 24.7 %collective-permute-done.14 = bf16[64,8192]{1,0:T(8,128)(2,1)S(1)} collective-permute-done((bf16[64,8192]{1,0:T(8,128)(2,1)S(1)}, bf16[64,8192]{1,0:T(8,128)(2,1)S(1)}, u32[]{:S(2)}, u32[]{:S(2)}) %collective-permute-start.14) | collective-permute-done | bytes 1048608 | tf_op jit(solution)/shard_map/ppermute | solution.py:10
  750.2 1.4 fusion.23
  752.4 1.4 multiply_convert_fusion
  755.0 1.6 collective-permute-start.16
  757.8 3.0 collective-permute-done.17
  761.8 4.9 fusion
  766.8 131.6 %reduce-scatter.11.cloned.1.call-done = f32[64,128]{1,0:T(8,128)} async-done(((f32[64,8192]{1,0:T(8,128)}), f32[64,128]{1,0:T(8,128)}) %reduce-scatter.11.cloned.1.call-update) | async-done | bytes 32784 | tf_op jit(solution)/shard_map/reduce_scatter | solution.py:94
  899.4 41.5 %all_to_all.23 = bf16[64,64,128]{2,1,0:T(8,128)(2,1)S(1)} all-to-all(bf16[64,64,128]{2,1,0:T(8,128)(2,1)S(1)} %stack.71), channel_id=1, replica_groups=mesh['section'=4,'tp'=64] {'tp'}, dimensions={0} | all-to-all | bytes 2097152 | tf_op jit(solution)/shard_map/all_to_all | solution.py:97
  943.1 25.1 %collective-permute-done.18 = bf16[64,8192]{1,0:T(8,128)(2,1)} collective-permute-done((bf16[64,8192]{1,0:T(8,128)(2,1)}, bf16[64,8192]{1,0:T(8,128)(2,1)}, u32[]{:S(2)}, u32[]{:S(2)}) %collective-permute-start.18) | collective-permute-done | bytes 1048608 | tf_op jit(solution)/shard_map/ppermute | solution.py:10
  968.3 1.3 select_bitcast_fusion
  (136 shorter events, 26.8 us)
Async XLA Ops:
  6.5 78.0 %all-gather.2.cloned.1.call-start = ((), (), s32[]{:S(2)}) async-start(), calls=%async_computation.8 | async-start | bytes 1064960 | tf_op jit(solution)/shard_map/all_gather | solution.py:64
  6.5 31.1 %collective-permute-start = (s32[4]{0:T(128)}, s32[4]{0:T(128)S(1)}, u32[]{:S(2)}, u32[]{:S(2)}) collective-permute-start(s32[4]{0:T(128)} %bitcast.195), channel_id=1, source_target_pairs={{63,0},{0,1},{1,2},{2,3},{3,4},{4,5},{5,6},{6,7},{7,8},{8,9},{9,10... | collective-permute-start | bytes 56 | tf_op jit(solution)/shard_map/ppermute | solution.py:10
  9.6 30.2 %collective-permute-start.2 = (s32[4]{0:T(128)}, s32[4]{0:T(128)S(1)}, u32[]{:S(2)}, u32[]{:S(2)}) collective-permute-start(s32[4]{0:T(128)} %bitcast.196), channel_id=1, source_target_pairs={{62,0},{63,1},{0,2},{1,3},{2,4},{3,5},{4,6},{5,7},{6,8},{7,9},{8,1... | collective-permute-start | bytes 56 | tf_op jit(solution)/shard_map/ppermute | solution.py:10
  11.2 30.7 %collective-permute-start.4 = (s32[4]{0:T(128)}, s32[4]{0:T(128)S(1)}, u32[]{:S(2)}, u32[]{:S(2)}) collective-permute-start(s32[4]{0:T(128)} %bitcast.197), channel_id=1, source_target_pairs={{61,0},{62,1},{63,2},{0,3},{1,4},{2,5},{3,6},{4,7},{5,8},{6,9},{7,... | collective-permute-start | bytes 56 | tf_op jit(solution)/shard_map/ppermute | solution.py:10
  12.9 233.4 %reduce-scatter.5.cloned.1.call-start = ((), (), s32[]{:S(2)}) async-start(), calls=%async_computation.9 | async-start | bytes 2129920 | tf_op jit(solution)/shard_map/reduce_scatter | solution.py:94
  16.4 6.4 copy-start.11
  23.1 6.5 copy-start.12
  30.5 4.6 copy-start.7
  35.1 2.3 copy-start.10
  35.1 2.5 copy-start.13
  35.1 51.0 %copy-start.9 = (f32[1,8192]{1,0:T(1,128)S(1)}, f32[1,8192]{1,0:T(1,128)}, u32[]{:S(2)}) copy-start(f32[1,8192]{1,0:T(1,128)} %param.10) | copy-start | bytes 98308
  86.1 4.1 copy-start.3
  86.1 4.1 copy-start.8
  92.0 17.5 %collective-permute-start.1 = (bf16[1,4096]{1,0:T(2,128)(2,1)S(1)}, bf16[1,4096]{1,0:T(2,128)(2,1)S(1)}, u32[]{:S(2)}, u32[]{:S(2)}) collective-permute-start(bf16[1,4096]{1,0:T(2,128)(2,1)S(1)} %get-tuple-element.198), channel_id=1, source_target_pairs={{1,0},{2,1},{3,2},{4,3},{5,4},{6,5},{7,6},{8,7},{9,8},{10,9},{11,1... | collective-permute-start | bytes 24584 | tf_op jit(solution)/shard_map/ppermute | solution.py:10
  92.3 17.2 %collective-permute-start.3 = (bf16[1,4096]{1,0:T(2,128)(2,1)S(1)}, bf16[1,4096]{1,0:T(2,128)(2,1)S(1)}, u32[]{:S(2)}, u32[]{:S(2)}) collective-permute-start(bf16[1,4096]{1,0:T(2,128)(2,1)S(1)} %get-tuple-element.197), channel_id=1, source_target_pairs={{2,0},{3,1},{4,2},{5,3},{6,4},{7,5},{8,6},{9,7},{10,8},{11,9},{12,... | collective-permute-start | bytes 24584 | tf_op jit(solution)/shard_map/ppermute | solution.py:10
  96.6 12.9 %collective-permute-start.5 = (bf16[1,4096]{1,0:T(2,128)(2,1)S(1)}, bf16[1,4096]{1,0:T(2,128)(2,1)S(1)}, u32[]{:S(2)}, u32[]{:S(2)}) collective-permute-start(bf16[1,4096]{1,0:T(2,128)(2,1)S(1)} %get-tuple-element.196), channel_id=1, source_target_pairs={{3,0},{4,1},{5,2},{6,3},{7,4},{8,5},{9,6},{10,7},{11,8},{12,9},{13... | collective-permute-start | bytes 24584 | tf_op jit(solution)/shard_map/ppermute | solution.py:10
  115.5 348.0 %reduce-scatter.7.cloned.1.call-start = ((), (), s32[]{:S(2)}) async-start(), calls=%async_computation.10 | async-start | bytes 2129920 | tf_op jit(solution)/shard_map/reduce_scatter | solution.py:94
  247.3 67.9 %copy-start = (bf16[8192,256]{0,1:T(8,128)(2,1)S(1)}, bf16[8192,256]{0,1:T(8,128)(2,1)}, u32[]{:S(2)}) copy-start(bf16[8192,256]{0,1:T(8,128)(2,1)} %bitcast_multiply_fusion.2) | copy-start | bytes 12582916
  288.9 26.0 %collective-permute-start.6 = (bf16[64,8192]{1,0:T(8,128)(2,1)S(1)}, bf16[64,8192]{1,0:T(8,128)(2,1)S(1)}, u32[]{:S(2)}, u32[]{:S(2)}) collective-permute-start(bf16[64,8192]{1,0:T(8,128)(2,1)S(1)} %copy_bitcast_fusion.3), channel_id=1, source_target_pairs={{192,0},{0,64},{64,128},{128,192},{193,1},{1,65},{65,129},{129,193... | collective-permute-start | bytes 3145736 | tf_op jit(solution)/shard_map/ppermute | solution.py:10
  315.3 2.2 copy-start.4
  319.2 3.7 collective-permute-start.7
  320.1 2.7 collective-permute-start.8
  321.8 4.1 collective-permute-start.9
  331.9 349.1 %reduce-scatter.9.cloned.1.call-start = ((), (), s32[]{:S(2)}) async-start(), calls=%async_computation.11 | async-start | bytes 2129920 | tf_op jit(solution)/shard_map/reduce_scatter | solution.py:94
  464.5 68.2 %copy-start.1 = (bf16[8192,256]{0,1:T(8,128)(2,1)S(1)}, bf16[8192,256]{0,1:T(8,128)(2,1)}, u32[]{:S(2)}) copy-start(bf16[8192,256]{0,1:T(8,128)(2,1)} %bitcast_multiply_fusion.2) | copy-start | bytes 12582916
  506.3 26.0 %collective-permute-start.10 = (bf16[64,8192]{1,0:T(8,128)(2,1)S(1)}, bf16[64,8192]{1,0:T(8,128)(2,1)S(1)}, u32[]{:S(2)}, u32[]{:S(2)}) collective-permute-start(bf16[64,8192]{1,0:T(8,128)(2,1)S(1)} %copy_bitcast_fusion.2), channel_id=1, source_target_pairs={{192,0},{0,64},{64,128},{128,192},{193,1},{1,65},{65,129},{129,193... | collective-permute-start | bytes 3145736 | tf_op jit(solution)/shard_map/ppermute | solution.py:10
  532.6 2.2 copy-start.5
  536.6 3.9 collective-permute-start.11
  537.7 2.7 collective-permute-start.12
  539.4 4.1 collective-permute-start.13
  549.4 348.9 %reduce-scatter.11.cloned.1.call-start = ((), (), s32[]{:S(2)}) async-start(), calls=%async_computation.12 | async-start | bytes 2129920 | tf_op jit(solution)/shard_map/reduce_scatter | solution.py:94
  682.0 68.1 %copy-start.2 = (bf16[8192,256]{0,1:T(8,128)(2,1)S(1)}, bf16[8192,256]{0,1:T(8,128)(2,1)}, u32[]{:S(2)}) copy-start(bf16[8192,256]{0,1:T(8,128)(2,1)} %bitcast_multiply_fusion.2) | copy-start | bytes 12582916
  723.8 26.0 %collective-permute-start.14 = (bf16[64,8192]{1,0:T(8,128)(2,1)S(1)}, bf16[64,8192]{1,0:T(8,128)(2,1)S(1)}, u32[]{:S(2)}, u32[]{:S(2)}) collective-permute-start(bf16[64,8192]{1,0:T(8,128)(2,1)S(1)} %copy_bitcast_fusion.1), channel_id=1, source_target_pairs={{192,0},{0,64},{64,128},{128,192},{193,1},{1,65},{65,129},{129,193... | collective-permute-start | bytes 3145736 | tf_op jit(solution)/shard_map/ppermute | solution.py:10
  750.2 2.2 copy-start.6
  754.1 3.7 collective-permute-start.15
  755.0 2.7 collective-permute-start.16
  756.7 4.1 collective-permute-start.17
  942.0 26.3 %collective-permute-start.18 = (bf16[64,8192]{1,0:T(8,128)(2,1)}, bf16[64,8192]{1,0:T(8,128)(2,1)}, u32[]{:S(2)}, u32[]{:S(2)}) collective-permute-start(bf16[64,8192]{1,0:T(8,128)(2,1)} %copy_bitcast_fusion), channel_id=1, source_target_pairs={{192,0},{0,64},{64,128},{128,192},{193,1},{1,65},{65,129},{129,193... | collective-permute-start | bytes 3145736 | tf_op jit(solution)/shard_map/ppermute | solution.py:10
Sparse Core Ops, SparseCore 0:
  13.0 71.5 all-gather.1
  115.6 130.6 reduce-scatter.4
  332.0 131.4 reduce-scatter.6
  549.6 131.3 reduce-scatter.8
  766.9 131.4 reduce-scatter.10
